TPU v7x, 256 devices: a whole 4x4x8 slice. The times are simulated.
256 devices in a mesh: seq: 32 (over y, z), head: 8 (over x, core).
Axes of the slice: x: 4, y: 4, z: 8, core: 2. Of those that a mesh axis runs over, the one named last changes fastest.
Arguments:
- tokens: bfloat16 [32768, 4096], P('seq'), may hold values from -50 to 50
- norm_gain: float32 [4096], replicated, may hold values from 0.1 to 1.9
- wq: bfloat16 [4096, 4096], P('seq', 'head'), may hold values from -2.34375 to 2.34375
- wk: bfloat16 [4096, 1024], P('seq', 'head'), may hold values from -0.09375 to 0.09375
- wv: bfloat16 [4096, 1024], P('seq', 'head'), may hold values from -0.09375 to 0.09375
- wo: bfloat16 [4096, 4096], P('head', 'seq'), may hold values from -0.1875 to 0.1875
- gate_bias: float32 [32], P('head'), may hold values from -3 to 3
- mem_init: float32 [8, 128, 128], P('head'), may hold values from -32768 to 32768
- norm_init: float32 [8, 128], P('head'), may hold values from 512 to 2048
Outputs:
- attended: bfloat16 [32768, 4096], P('seq', 'head')
All inputs are finite; a program needn't handle non-finite values.
Results may differ from a plain program's by a relative error of at most 0.018.
Values may be sent and summed in bfloat16 or wider, within the bound.
No kernel may reach another device: no remote copies, remote signals or barrier semaphores. Data moves between devices by JAX's collectives and lax.ppermute only.
A program may use at most 128 MiB of HBM per device.

v0:
```python
import math
import jax
import jax.numpy as jnp
from jax import lax
from jax.sharding import PartitionSpec as P

H = 32
KVH = 8
HD = 128
SEG = 512


def from_behind(block, axis, distance):
    devices = range(lax.axis_size(axis))
    route = [(i - distance, i) for i in devices if i - distance in devices]
    return lax.ppermute(block, axis, route)


def feature_map(values_in):
    return jnp.where(values_in > 0, values_in + 1.0, jnp.exp(jnp.minimum(values_in, 0.0)))


def per_device(tokens, norm_gain, wq, wk, wv, wo, gate_bias, mem_init, norm_init):
    highest = lax.Precision.HIGHEST
    widened = tokens.astype(jnp.float32)
    normed = (
        widened * lax.rsqrt(jnp.mean(widened * widened, axis=-1, keepdims=True) + 1e-05) * norm_gain
    ).astype(jnp.bfloat16)
    token_count = normed.shape[0]

    def project(shard_piece):
        return jnp.dot(normed, shard_piece, preferred_element_type=jnp.float32)

    query_wide = project(lax.all_gather(wq, "seq", axis=0, tiled=True))
    key_wide = project(lax.all_gather(wk, "seq", axis=0, tiled=True))
    value_wide = project(lax.all_gather(wv, "seq", axis=0, tiled=True))
    queries = query_wide.astype(jnp.bfloat16)
    keys_all = key_wide.astype(jnp.bfloat16)
    values_all = value_wide.astype(jnp.bfloat16)
    group = H // KVH
    kv_local = wk.shape[1] // HD
    segments = token_count // SEG
    query_seg = queries.reshape(segments, SEG, kv_local, group, HD)
    key_seg = keys_all.reshape(segments, SEG, kv_local, HD)
    value_seg = values_all.reshape(segments, SEG, kv_local, HD)
    key_feats = feature_map(key_seg.astype(jnp.float32))
    delta_mem = jnp.einsum(
        "nski,nskj->nkij", key_feats, value_seg.astype(jnp.float32), precision=highest
    )
    delta_norm = jnp.sum(key_feats, axis=1)
    own_mem = jnp.sum(delta_mem, axis=0)
    own_norm = jnp.sum(delta_norm, axis=0)
    zero_mem = jnp.zeros_like(own_mem)
    zero_norm = jnp.zeros_like(own_norm)

    def pass_along(step_index, carried):
        return (
            from_behind((carried[0] + own_mem).astype(jnp.bfloat16), "seq", 1).astype(jnp.float32),
            from_behind((carried[1] + own_norm).astype(jnp.bfloat16), "seq", 1).astype(jnp.float32),
        )

    carried_mem, carried_norm = lax.fori_loop(
        0, lax.axis_size("seq") - 1, pass_along, (zero_mem, zero_norm)
    )
    inner_mem = jnp.concatenate([zero_mem[None], jnp.cumsum(delta_mem, axis=0)[:-1]], axis=0)
    inner_norm = jnp.concatenate([zero_norm[None], jnp.cumsum(delta_norm, axis=0)[:-1]], axis=0)
    mem_before = mem_init[None] + carried_mem[None] + inner_mem
    norm_before = norm_init[None] + carried_norm[None] + inner_norm
    query_feats = feature_map(query_seg.astype(jnp.float32))
    numer = jnp.einsum("nskgi,nkij->nskgj", query_feats, mem_before, precision=highest)
    denom = jnp.einsum("nskgi,nki->nskg", query_feats, norm_before, precision=highest)
    retrieved = numer / denom[..., None]
    score_scale = 1.0 / math.sqrt(HD)
    causal = lax.broadcasted_iota(jnp.int32, (SEG, SEG), 0) >= lax.broadcasted_iota(
        jnp.int32, (SEG, SEG), 1
    )
    scores = (
        jnp.einsum("nqkgd,nskd->nkgqs", query_seg, key_seg, preferred_element_type=jnp.float32)
        * score_scale
    )
    scores = jnp.where(causal, scores, -1e30)
    peak = jnp.max(scores, axis=-1, keepdims=True)
    expd = jnp.exp(scores - peak)
    probs = (expd / jnp.sum(expd, axis=-1, keepdims=True)).astype(jnp.bfloat16)
    local = jnp.einsum("nkgqs,nskd->nqkgd", probs, value_seg, preferred_element_type=jnp.float32)
    gate_mix = jax.nn.sigmoid(gate_bias).reshape(kv_local, group)
    mixed = (
        gate_mix[None, None, :, :, None] * retrieved
        + (1.0 - gate_mix)[None, None, :, :, None] * local
    )
    mixed = mixed.astype(jnp.bfloat16).reshape(token_count, kv_local * group * HD)
    partial_out = jnp.dot(
        mixed, lax.all_gather(wo, "seq", axis=1, tiled=True), preferred_element_type=jnp.float32
    )
    return lax.psum_scatter(
        partial_out.astype(jnp.bfloat16), "head", scatter_dimension=1, tiled=True
    )


def solution(mesh):
    placed = (
        P("seq", None),
        P(),
        P("seq", "head"),
        P("seq", "head"),
        P("seq", "head"),
        P("head", "seq"),
        P("head"),
        P("head", None, None),
        P("head", None),
    )
    return jax.shard_map(
        per_device, mesh=mesh, in_specs=placed, out_specs=P("seq", "head"), check_vma=False
    )
```

profile of v0, /device:TPU:1, one launch (start us, length us, event | category | flops | bytes accessed | tf_op | source)
XLA Modules:
  0.0 559.1 jit_solution(2536971388080526449)
XLA Ops:
  9.5 5.1 fusion.3
  15.2 10.3 %fusion.5 = bf16[1024,4096]{1,0:T(8,128)(2,1)} fusion(bf16[1024,4096]{1,0:T(8,128)(2,1)} %param.11, f32[4096]{0:T(1024)S(1)} %copy-done.2, f32[1024]{0:T(1024)S(1)} %add_rsqrt_fusion), kind=kLoop, calls=%fused_computation.9 | loop fusion | flops 16777216 | bytes 16797696 | tf_op jit(solution)/shard_map/convert_element_type | solution.py:28
  25.5 60.1 %all-gather.5.cloned.1.call-done = bf16[4096,128]{1,0:T(8,128)(2,1)} async-done(((bf16[128,128]{1,0:T(8,128)(2,1)}), bf16[4096,128]{1,0:T(8,128)(2,1)}) %all-gather.5.cloned.1.call-update) | async-done | bytes 1048592 | tf_op jit(solution)/shard_map/all_gather | solution.py:35
  85.6 6.0 %fusion.38 = (f32[128]{0:T(128)S(1)}, bf16[1024,128]{1,0:T(8,128)(2,1)S(1)}) fusion(bf16[1024,4096]{1,0:T(8,128)(2,1)} %fusion.5, bf16[4096,128]{1,0:T(8,128)(2,1)} %all-gather.5.cloned.1.call-done), kind=kOutput, calls=%fused_computation.57 | convolution fusion | flops 1074659200 | bytes 9699840 | tf_op jit(solution)/shard_map/dot_general | solution.py:32
  91.7 70.3 %all-gather.7.cloned.1.call-done = bf16[4096,128]{1,0:T(8,128)(2,1)} async-done(((bf16[128,128]{1,0:T(8,128)(2,1)}), bf16[4096,128]{1,0:T(8,128)(2,1)}) %all-gather.7.cloned.1.call-update) | async-done | bytes 1048592 | tf_op jit(solution)/shard_map/all_gather | solution.py:36
  162.0 5.9 %convolution_convert_fusion.2 = bf16[1024,128]{1,0:T(8,128)(2,1)S(1)} fusion(bf16[1024,4096]{1,0:T(8,128)(2,1)} %fusion.5, bf16[4096,128]{1,0:T(8,128)(2,1)} %all-gather.7.cloned.1.call-done), kind=kOutput, calls=%fused_computation.32 | convolution fusion | flops 1073872896 | bytes 9699328 | tf_op jit(solution)/shard_map/dot_general | solution.py:32
  168.9 253.9 %while.13 = (s32[]{:T(128)}, f32[1,128,128]{2,1,0:T(8,128)S(1)}, f32[1,128]{1,0:T(1,128)S(1)}, f32[1,128,128]{2,1,0:T(8,128)S(1)}, f32[1,128]{1,0:T(1,128)S(1)}, /*index=5*/s32[]{:T(128)}, s32[]{:T(128)}) while((s32[]{:T(128)}, f32[1,128,128]{2,1,0:T(8,128)S(1)}, f32[1,128]{1,0:T(1,128)S(1)}, f32[1,128,128]{2,1,0:T(8,128)S(1)}, ...), condition=%wide.region_4.5_spmd.clone, body=%wide.region_3.4_spmd.clone.sunk | while | flops 66051 | bytes 396456 | solution.py:62
  171.1 4.0 collective-permute-start.1
  182.2 4.0 collective-permute-start
  197.8 4.0 collective-permute-start
  221.2 4.0 collective-permute-start
  229.8 4.0 collective-permute-start
  233.8 4.0 collective-permute-start.1
  238.5 4.0 collective-permute-start
  246.9 4.0 collective-permute-start
  279.8 4.0 collective-permute-start
  292.2 4.0 collective-permute-start.1
  305.1 4.0 collective-permute-start
  313.5 4.0 collective-permute-start
  317.5 4.1 collective-permute-start.1
  322.4 4.0 collective-permute-start
  330.8 4.0 collective-permute-start
  334.8 4.4 collective-permute-start.1
  340.0 4.0 collective-permute-start
  367.7 4.3 collective-permute-start.1
  384.6 4.1 collective-permute-start.1
  401.3 4.0 collective-permute-start.1
  409.7 4.0 collective-permute-start.1
  418.1 4.0 collective-permute-start.1
  422.9 9.0 %convolution_convert_fusion.1 = bf16[1024,512]{1,0:T(8,128)(2,1)S(1)} fusion(bf16[1024,4096]{1,0:T(8,128)(2,1)} %fusion.5, bf16[4096,512]{1,0:T(8,128)(2,1)} %all-gather.9.cloned.1.call-done), kind=kOutput, calls=%fused_computation.31 | convolution fusion | flops 4295491584 | bytes 13631488 | tf_op jit(solution)/shard_map/dot_general | solution.py:32
  445.5 8.9 %convolution_convert_fusion = bf16[1024,4096]{1,0:T(8,128)(2,1)} fusion(bf16[512,4096]{1,0:T(8,128)(2,1)} %all-gather.11.cloned.1.call-done, bf16[128,8,4,128]{3,2,1,0:T(4,128)(2,1)S(1)} %bitcast.93), kind=kOutput, calls=%fused_computation.13 | convolution fusion | flops 4299161600 | bytes 13631488 | tf_op jit(solution)/shard_map/dot_general | solution.py:92
  454.5 98.1 %reduce-scatter.2.cloned.1.call-done = bf16[1024,512]{1,0:T(8,128)(2,1)} async-done(((bf16[1024,4096]{1,0:T(8,128)(2,1)}), bf16[1024,512]{1,0:T(8,128)(2,1)}) %reduce-scatter.2.cloned.1.call-update) | async-done | bytes 1048592 | tf_op jit(solution)/shard_map/reduce_scatter | solution.py:95
  (277 shorter events, 181.8 us)
Async XLA Ops:
  6.5 79.0 %all-gather.5.cloned.1.call-start = ((), (), s32[]{:S(2)}) async-start(), calls=%async_computation.1 | async-start | bytes 1081344 | tf_op jit(solution)/shard_map/all_gather | solution.py:35
  7.3 154.7 %all-gather.7.cloned.1.call-start = ((), (), s32[]{:S(2)}) async-start(), calls=%async_computation.2 | async-start | bytes 1081344 | tf_op jit(solution)/shard_map/all_gather | solution.py:36
  8.0 414.9 %all-gather.9.cloned.1.call-start = ((), (), s32[]{:S(2)}) async-start(), calls=%async_computation.3 | async-start | bytes 4325376 | tf_op jit(solution)/shard_map/all_gather | solution.py:34
  8.7 436.8 %all-gather.11.cloned.1.call-start = ((), (), s32[]{:S(2)}) async-start(), calls=%async_computation.4 | async-start | bytes 4325376 | tf_op jit(solution)/shard_map/all_gather | solution.py:93
  9.3 543.3 %reduce-scatter.2.cloned.1.call-start = ((), (), s32[]{:S(2)}) async-start(), calls=%async_computation.5 | async-start | bytes 9437184 | tf_op jit(solution)/shard_map/reduce_scatter | solution.py:95
  182.2 8.1 %collective-permute-start = (bf16[1,128,128]{2,1,0:T(8,128)(2,1)S(1)}, bf16[1,128,128]{2,1,0:T(8,128)(2,1)S(1)}, u32[]{:S(2)}, u32[]{:S(2)}) collective-permute-start(bf16[1,128,128]{2,1,0:T(8,128)(2,1)S(1)} %fusion.74), channel_id=1, source_target_pairs={{0,8},{8,16},{16,24},{24,32},{32,40},{40,48},{48,56},{56,64},{64,7... | collective-permute-start | bytes 98312 | tf_op jit(solution)/shard_map/while/body/eval_jaxpr/ppermute | solution.py:16
  197.8 8.1 %collective-permute-start = (bf16[1,128,128]{2,1,0:T(8,128)(2,1)S(1)}, bf16[1,128,128]{2,1,0:T(8,128)(2,1)S(1)}, u32[]{:S(2)}, u32[]{:S(2)}) collective-permute-start(bf16[1,128,128]{2,1,0:T(8,128)(2,1)S(1)} %fusion.74), channel_id=1, source_target_pairs={{0,8},{8,16},{16,24},{24,32},{32,40},{40,48},{48,56},{56,64},{64,7... | collective-permute-start | bytes 98312 | tf_op jit(solution)/shard_map/while/body/eval_jaxpr/ppermute | solution.py:16
  205.9 7.8 %collective-permute-start = (bf16[1,128,128]{2,1,0:T(8,128)(2,1)S(1)}, bf16[1,128,128]{2,1,0:T(8,128)(2,1)S(1)}, u32[]{:S(2)}, u32[]{:S(2)}) collective-permute-start(bf16[1,128,128]{2,1,0:T(8,128)(2,1)S(1)} %fusion.74), channel_id=1, source_target_pairs={{0,8},{8,16},{16,24},{24,32},{32,40},{40,48},{48,56},{56,64},{64,7... | collective-permute-start | bytes 98312 | tf_op jit(solution)/shard_map/while/body/eval_jaxpr/ppermute | solution.py:16
  221.2 8.5 %collective-permute-start = (bf16[1,128,128]{2,1,0:T(8,128)(2,1)S(1)}, bf16[1,128,128]{2,1,0:T(8,128)(2,1)S(1)}, u32[]{:S(2)}, u32[]{:S(2)}) collective-permute-start(bf16[1,128,128]{2,1,0:T(8,128)(2,1)S(1)} %fusion.74), channel_id=1, source_target_pairs={{0,8},{8,16},{16,24},{24,32},{32,40},{40,48},{48,56},{56,64},{64,7... | collective-permute-start | bytes 98312 | tf_op jit(solution)/shard_map/while/body/eval_jaxpr/ppermute | solution.py:16
  229.8 8.7 %collective-permute-start = (bf16[1,128,128]{2,1,0:T(8,128)(2,1)S(1)}, bf16[1,128,128]{2,1,0:T(8,128)(2,1)S(1)}, u32[]{:S(2)}, u32[]{:S(2)}) collective-permute-start(bf16[1,128,128]{2,1,0:T(8,128)(2,1)S(1)} %fusion.74), channel_id=1, source_target_pairs={{0,8},{8,16},{16,24},{24,32},{32,40},{40,48},{48,56},{56,64},{64,7... | collective-permute-start | bytes 98312 | tf_op jit(solution)/shard_map/while/body/eval_jaxpr/ppermute | solution.py:16
  238.5 8.3 %collective-permute-start = (bf16[1,128,128]{2,1,0:T(8,128)(2,1)S(1)}, bf16[1,128,128]{2,1,0:T(8,128)(2,1)S(1)}, u32[]{:S(2)}, u32[]{:S(2)}) collective-permute-start(bf16[1,128,128]{2,1,0:T(8,128)(2,1)S(1)} %fusion.74), channel_id=1, source_target_pairs={{0,8},{8,16},{16,24},{24,32},{32,40},{40,48},{48,56},{56,64},{64,7... | collective-permute-start | bytes 98312 | tf_op jit(solution)/shard_map/while/body/eval_jaxpr/ppermute | solution.py:16
  246.9 8.3 %collective-permute-start = (bf16[1,128,128]{2,1,0:T(8,128)(2,1)S(1)}, bf16[1,128,128]{2,1,0:T(8,128)(2,1)S(1)}, u32[]{:S(2)}, u32[]{:S(2)}) collective-permute-start(bf16[1,128,128]{2,1,0:T(8,128)(2,1)S(1)} %fusion.74), channel_id=1, source_target_pairs={{0,8},{8,16},{16,24},{24,32},{32,40},{40,48},{48,56},{56,64},{64,7... | collective-permute-start | bytes 98312 | tf_op jit(solution)/shard_map/while/body/eval_jaxpr/ppermute | solution.py:16
  255.2 8.3 %collective-permute-start = (bf16[1,128,128]{2,1,0:T(8,128)(2,1)S(1)}, bf16[1,128,128]{2,1,0:T(8,128)(2,1)S(1)}, u32[]{:S(2)}, u32[]{:S(2)}) collective-permute-start(bf16[1,128,128]{2,1,0:T(8,128)(2,1)S(1)} %fusion.74), channel_id=1, source_target_pairs={{0,8},{8,16},{16,24},{24,32},{32,40},{40,48},{48,56},{56,64},{64,7... | collective-permute-start | bytes 98312 | tf_op jit(solution)/shard_map/while/body/eval_jaxpr/ppermute | solution.py:16
  263.6 8.3 %collective-permute-start = (bf16[1,128,128]{2,1,0:T(8,128)(2,1)S(1)}, bf16[1,128,128]{2,1,0:T(8,128)(2,1)S(1)}, u32[]{:S(2)}, u32[]{:S(2)}) collective-permute-start(bf16[1,128,128]{2,1,0:T(8,128)(2,1)S(1)} %fusion.74), channel_id=1, source_target_pairs={{0,8},{8,16},{16,24},{24,32},{32,40},{40,48},{48,56},{56,64},{64,7... | collective-permute-start | bytes 98312 | tf_op jit(solution)/shard_map/while/body/eval_jaxpr/ppermute | solution.py:16
  271.9 7.8 %collective-permute-start = (bf16[1,128,128]{2,1,0:T(8,128)(2,1)S(1)}, bf16[1,128,128]{2,1,0:T(8,128)(2,1)S(1)}, u32[]{:S(2)}, u32[]{:S(2)}) collective-permute-start(bf16[1,128,128]{2,1,0:T(8,128)(2,1)S(1)} %fusion.74), channel_id=1, source_target_pairs={{0,8},{8,16},{16,24},{24,32},{32,40},{40,48},{48,56},{56,64},{64,7... | collective-permute-start | bytes 98312 | tf_op jit(solution)/shard_map/while/body/eval_jaxpr/ppermute | solution.py:16
  279.8 8.6 %collective-permute-start = (bf16[1,128,128]{2,1,0:T(8,128)(2,1)S(1)}, bf16[1,128,128]{2,1,0:T(8,128)(2,1)S(1)}, u32[]{:S(2)}, u32[]{:S(2)}) collective-permute-start(bf16[1,128,128]{2,1,0:T(8,128)(2,1)S(1)} %fusion.74), channel_id=1, source_target_pairs={{0,8},{8,16},{16,24},{24,32},{32,40},{40,48},{48,56},{56,64},{64,7... | collective-permute-start | bytes 98312 | tf_op jit(solution)/shard_map/while/body/eval_jaxpr/ppermute | solution.py:16
  288.5 8.5 %collective-permute-start = (bf16[1,128,128]{2,1,0:T(8,128)(2,1)S(1)}, bf16[1,128,128]{2,1,0:T(8,128)(2,1)S(1)}, u32[]{:S(2)}, u32[]{:S(2)}) collective-permute-start(bf16[1,128,128]{2,1,0:T(8,128)(2,1)S(1)} %fusion.74), channel_id=1, source_target_pairs={{0,8},{8,16},{16,24},{24,32},{32,40},{40,48},{48,56},{56,64},{64,7... | collective-permute-start | bytes 98312 | tf_op jit(solution)/shard_map/while/body/eval_jaxpr/ppermute | solution.py:16
  297.0 8.0 %collective-permute-start = (bf16[1,128,128]{2,1,0:T(8,128)(2,1)S(1)}, bf16[1,128,128]{2,1,0:T(8,128)(2,1)S(1)}, u32[]{:S(2)}, u32[]{:S(2)}) collective-permute-start(bf16[1,128,128]{2,1,0:T(8,128)(2,1)S(1)} %fusion.74), channel_id=1, source_target_pairs={{0,8},{8,16},{16,24},{24,32},{32,40},{40,48},{48,56},{56,64},{64,7... | collective-permute-start | bytes 98312 | tf_op jit(solution)/shard_map/while/body/eval_jaxpr/ppermute | solution.py:16
  305.1 8.4 %collective-permute-start = (bf16[1,128,128]{2,1,0:T(8,128)(2,1)S(1)}, bf16[1,128,128]{2,1,0:T(8,128)(2,1)S(1)}, u32[]{:S(2)}, u32[]{:S(2)}) collective-permute-start(bf16[1,128,128]{2,1,0:T(8,128)(2,1)S(1)} %fusion.74), channel_id=1, source_target_pairs={{0,8},{8,16},{16,24},{24,32},{32,40},{40,48},{48,56},{56,64},{64,7... | collective-permute-start | bytes 98312 | tf_op jit(solution)/shard_map/while/body/eval_jaxpr/ppermute | solution.py:16
  313.5 8.8 %collective-permute-start = (bf16[1,128,128]{2,1,0:T(8,128)(2,1)S(1)}, bf16[1,128,128]{2,1,0:T(8,128)(2,1)S(1)}, u32[]{:S(2)}, u32[]{:S(2)}) collective-permute-start(bf16[1,128,128]{2,1,0:T(8,128)(2,1)S(1)} %fusion.74), channel_id=1, source_target_pairs={{0,8},{8,16},{16,24},{24,32},{32,40},{40,48},{48,56},{56,64},{64,7... | collective-permute-start | bytes 98312 | tf_op jit(solution)/shard_map/while/body/eval_jaxpr/ppermute | solution.py:16
  322.4 8.4 %collective-permute-start = (bf16[1,128,128]{2,1,0:T(8,128)(2,1)S(1)}, bf16[1,128,128]{2,1,0:T(8,128)(2,1)S(1)}, u32[]{:S(2)}, u32[]{:S(2)}) collective-permute-start(bf16[1,128,128]{2,1,0:T(8,128)(2,1)S(1)} %fusion.74), channel_id=1, source_target_pairs={{0,8},{8,16},{16,24},{24,32},{32,40},{40,48},{48,56},{56,64},{64,7... | collective-permute-start | bytes 98312 | tf_op jit(solution)/shard_map/while/body/eval_jaxpr/ppermute | solution.py:16
  330.8 9.1 %collective-permute-start = (bf16[1,128,128]{2,1,0:T(8,128)(2,1)S(1)}, bf16[1,128,128]{2,1,0:T(8,128)(2,1)S(1)}, u32[]{:S(2)}, u32[]{:S(2)}) collective-permute-start(bf16[1,128,128]{2,1,0:T(8,128)(2,1)S(1)} %fusion.74), channel_id=1, source_target_pairs={{0,8},{8,16},{16,24},{24,32},{32,40},{40,48},{48,56},{56,64},{64,7... | collective-permute-start | bytes 98312 | tf_op jit(solution)/shard_map/while/body/eval_jaxpr/ppermute | solution.py:16
  340.0 8.3 %collective-permute-start = (bf16[1,128,128]{2,1,0:T(8,128)(2,1)S(1)}, bf16[1,128,128]{2,1,0:T(8,128)(2,1)S(1)}, u32[]{:S(2)}, u32[]{:S(2)}) collective-permute-start(bf16[1,128,128]{2,1,0:T(8,128)(2,1)S(1)} %fusion.74), channel_id=1, source_target_pairs={{0,8},{8,16},{16,24},{24,32},{32,40},{40,48},{48,56},{56,64},{64,7... | collective-permute-start | bytes 98312 | tf_op jit(solution)/shard_map/while/body/eval_jaxpr/ppermute | solution.py:16
  348.3 7.7 %collective-permute-start = (bf16[1,128,128]{2,1,0:T(8,128)(2,1)S(1)}, bf16[1,128,128]{2,1,0:T(8,128)(2,1)S(1)}, u32[]{:S(2)}, u32[]{:S(2)}) collective-permute-start(bf16[1,128,128]{2,1,0:T(8,128)(2,1)S(1)} %fusion.74), channel_id=1, source_target_pairs={{0,8},{8,16},{16,24},{24,32},{32,40},{40,48},{48,56},{56,64},{64,7... | collective-permute-start | bytes 98312 | tf_op jit(solution)/shard_map/while/body/eval_jaxpr/ppermute | solution.py:16
  356.1 8.0 %collective-permute-start = (bf16[1,128,128]{2,1,0:T(8,128)(2,1)S(1)}, bf16[1,128,128]{2,1,0:T(8,128)(2,1)S(1)}, u32[]{:S(2)}, u32[]{:S(2)}) collective-permute-start(bf16[1,128,128]{2,1,0:T(8,128)(2,1)S(1)} %fusion.74), channel_id=1, source_target_pairs={{0,8},{8,16},{16,24},{24,32},{32,40},{40,48},{48,56},{56,64},{64,7... | collective-permute-start | bytes 98312 | tf_op jit(solution)/shard_map/while/body/eval_jaxpr/ppermute | solution.py:16
  364.1 8.6 %collective-permute-start = (bf16[1,128,128]{2,1,0:T(8,128)(2,1)S(1)}, bf16[1,128,128]{2,1,0:T(8,128)(2,1)S(1)}, u32[]{:S(2)}, u32[]{:S(2)}) collective-permute-start(bf16[1,128,128]{2,1,0:T(8,128)(2,1)S(1)} %fusion.74), channel_id=1, source_target_pairs={{0,8},{8,16},{16,24},{24,32},{32,40},{40,48},{48,56},{56,64},{64,7... | collective-permute-start | bytes 98312 | tf_op jit(solution)/shard_map/while/body/eval_jaxpr/ppermute | solution.py:16
  372.8 8.2 %collective-permute-start = (bf16[1,128,128]{2,1,0:T(8,128)(2,1)S(1)}, bf16[1,128,128]{2,1,0:T(8,128)(2,1)S(1)}, u32[]{:S(2)}, u32[]{:S(2)}) collective-permute-start(bf16[1,128,128]{2,1,0:T(8,128)(2,1)S(1)} %fusion.74), channel_id=1, source_target_pairs={{0,8},{8,16},{16,24},{24,32},{32,40},{40,48},{48,56},{56,64},{64,7... | collective-permute-start | bytes 98312 | tf_op jit(solution)/shard_map/while/body/eval_jaxpr/ppermute | solution.py:16
  381.0 8.4 %collective-permute-start = (bf16[1,128,128]{2,1,0:T(8,128)(2,1)S(1)}, bf16[1,128,128]{2,1,0:T(8,128)(2,1)S(1)}, u32[]{:S(2)}, u32[]{:S(2)}) collective-permute-start(bf16[1,128,128]{2,1,0:T(8,128)(2,1)S(1)} %fusion.74), channel_id=1, source_target_pairs={{0,8},{8,16},{16,24},{24,32},{32,40},{40,48},{48,56},{56,64},{64,7... | collective-permute-start | bytes 98312 | tf_op jit(solution)/shard_map/while/body/eval_jaxpr/ppermute | solution.py:16
  389.5 8.2 %collective-permute-start = (bf16[1,128,128]{2,1,0:T(8,128)(2,1)S(1)}, bf16[1,128,128]{2,1,0:T(8,128)(2,1)S(1)}, u32[]{:S(2)}, u32[]{:S(2)}) collective-permute-start(bf16[1,128,128]{2,1,0:T(8,128)(2,1)S(1)} %fusion.74), channel_id=1, source_target_pairs={{0,8},{8,16},{16,24},{24,32},{32,40},{40,48},{48,56},{56,64},{64,7... | collective-permute-start | bytes 98312 | tf_op jit(solution)/shard_map/while/body/eval_jaxpr/ppermute | solution.py:16
  397.8 8.3 %collective-permute-start = (bf16[1,128,128]{2,1,0:T(8,128)(2,1)S(1)}, bf16[1,128,128]{2,1,0:T(8,128)(2,1)S(1)}, u32[]{:S(2)}, u32[]{:S(2)}) collective-permute-start(bf16[1,128,128]{2,1,0:T(8,128)(2,1)S(1)} %fusion.74), channel_id=1, source_target_pairs={{0,8},{8,16},{16,24},{24,32},{32,40},{40,48},{48,56},{56,64},{64,7... | collective-permute-start | bytes 98312 | tf_op jit(solution)/shard_map/while/body/eval_jaxpr/ppermute | solution.py:16
  406.1 8.3 %collective-permute-start = (bf16[1,128,128]{2,1,0:T(8,128)(2,1)S(1)}, bf16[1,128,128]{2,1,0:T(8,128)(2,1)S(1)}, u32[]{:S(2)}, u32[]{:S(2)}) collective-permute-start(bf16[1,128,128]{2,1,0:T(8,128)(2,1)S(1)} %fusion.74), channel_id=1, source_target_pairs={{0,8},{8,16},{16,24},{24,32},{32,40},{40,48},{48,56},{56,64},{64,7... | collective-permute-start | bytes 98312 | tf_op jit(solution)/shard_map/while/body/eval_jaxpr/ppermute | solution.py:16
  414.5 8.3 %collective-permute-start = (bf16[1,128,128]{2,1,0:T(8,128)(2,1)S(1)}, bf16[1,128,128]{2,1,0:T(8,128)(2,1)S(1)}, u32[]{:S(2)}, u32[]{:S(2)}) collective-permute-start(bf16[1,128,128]{2,1,0:T(8,128)(2,1)S(1)} %fusion.74), channel_id=1, source_target_pairs={{0,8},{8,16},{16,24},{24,32},{32,40},{40,48},{48,56},{56,64},{64,7... | collective-permute-start | bytes 98312 | tf_op jit(solution)/shard_map/while/body/eval_jaxpr/ppermute | solution.py:16
  (44 other events, 1188.7 us)
Sparse Core Ops, SparseCore 0:
  10.0 75.5 all-gather.4
  88.2 73.7 all-gather.6
  164.6 81.8 all-gather.8
  248.8 82.8 all-gather.10
  454.6 97.9 reduce-scatter.1
where the time goes:
time: 565 us; the launch traced here: 559 us
  waiting for transfers between devices  253 us (45%)
  starting transfers between devices  230 us (41%)
  matrix products  40.5 us (7%)
  other arithmetic  19.2 us (3%)
  between operations  13.4 us (2%)
    ppermute x62, starting transfers between devices, from_behind(): return lax.ppermute(block, axis, route)  230 us
    reduce_scatter x1, waiting for transfers between devices, per_device(): lax.psum_scatter(partial_out.astype(jnp.bfloat16), 'head', scatter_dimens...  98.1 us
    all_gather x1, waiting for transfers between devices, per_device(): value_wide = project(lax.all_gather(wv, 'seq', axis=0, tiled=True))  70.3 us
    all_gather x1, waiting for transfers between devices, per_device(): key_wide = project(lax.all_gather(wk, 'seq', axis=0, tiled=True))  60.1 us
    ppermute x62, waiting for transfers between devices, from_behind(): return lax.ppermute(block, axis, route)  21.9 us
    dot_general x3, matrix products, project(): return jnp.dot(normed, shard_piece, preferred_element_type=jnp.float32)  20.9 us
  transfers between devices with their start and end apart: 67, of which 34 were waited for; matrix products, arithmetic and copies ran while one was open for 9% of the time, Pallas kernels for 0%

commit v1 on v0

--- a/solution.py
+++ b/solution.py
@@ -32,7 +32,9 @@
         return jnp.dot(normed, shard_piece, preferred_element_type=jnp.float32)
 
     query_wide = project(lax.all_gather(wq, "seq", axis=0, tiled=True))
-    key_wide = project(lax.all_gather(wk, "seq", axis=0, tiled=True))
+    key_wide = project(
+        jnp.concatenate(lax.all_to_all(jnp.stack([wk] * lax.axis_size("seq")), "seq", 0, 0), axis=0)
+    )
     value_wide = project(lax.all_gather(wv, "seq", axis=0, tiled=True))
     queries = query_wide.astype(jnp.bfloat16)
     keys_all = key_wide.astype(jnp.bfloat16)

time: 565 us -> 490 us (0.87)
  waiting for transfers between devices: 253 us -> 164 us
  starting transfers between devices: 230 us -> 242 us
    all_gather x1 -> x0, waiting for transfers between devices: 60.1 us -> none  [per_device(): key_wide = project(lax.all_gather(wk, 'seq', axis=0, tiled=True))]
    all_gather x1, waiting for transfers between devices: 70.3 us -> 33.1 us  [per_device(): value_wide = project(lax.all_gather(wv, 'seq', axis=0, tiled=True))]
    all_to_all x0 -> x1, starting transfers between devices: none -> 12 us  [per_device(): lax.all_to_all(jnp.stack([wk] * lax.axis_size('seq')), 'seq', 0, 0)]
    all_to_all x0 -> x1, waiting for transfers between devices: none -> 8.47 us  [per_device(): lax.all_to_all(jnp.stack([wk] * lax.axis_size('seq')), 'seq', 0, 0)]
  transfers between devices with their start and end apart: 67 -> 67, of which waited for: 34 -> 34; matrix products, arithmetic and copies ran while one was open for 9% -> 11% of each run, Pallas kernels for 0% -> 0%
where the time goes in v1:
time: 490 us; the launch traced here: 484 us
  starting transfers between devices  242 us (49%)
  waiting for transfers between devices  164 us (33%)
  matrix products  40.3 us (8%)
  other arithmetic  19.9 us (4%)
  between operations  13.4 us (3%)
    ppermute x62, starting transfers between devices, from_behind(): return lax.ppermute(block, axis, route)  230 us
    reduce_scatter x1, waiting for transfers between devices, per_device(): lax.psum_scatter(partial_out.astype(jnp.bfloat16), 'head', scatter_dimens...  98.1 us
    all_gather x1, waiting for transfers between devices, per_device(): value_wide = project(lax.all_gather(wv, 'seq', axis=0, tiled=True))  33.1 us
    ppermute x62, waiting for transfers between devices, from_behind(): return lax.ppermute(block, axis, route)  21.9 us
    dot_general x3, matrix products, project(): return jnp.dot(normed, shard_piece, preferred_element_type=jnp.float32)  20.7 us
    all_to_all x1, starting transfers between devices, per_device(): lax.all_to_all(jnp.stack([wk] * lax.axis_size('seq')), 'seq', 0, 0)  12 us
    convert_element_type x1, other arithmetic, per_device(): normed = (widened * lax.rsqrt(jnp.mean(widened * widened, axis=-1, keepdi...  10.3 us
  transfers between devices with their start and end apart: 67, of which 34 were waited for; matrix products, arithmetic and copies ran while one was open for 11% of the time, Pallas kernels for 0%

profile of v1, /device:TPU:1, one launch (start us, length us, event | category | flops | bytes accessed | tf_op | source)
XLA Modules:
  0.0 484.2 jit_solution(9521950406188183402)
XLA Ops:
  10.0 12.0 %all-to-all-start = ((bf16[32,128,128]{2,1,0:T(8,128)(2,1)}), bf16[32,128,128]{2,1,0:T(8,128)(2,1)S(1)}, u32[]{:S(2)}, u32[]{:S(2)}) async-start(bf16[32,128,128]{2,1,0:T(8,128)(2,1)} %stack.2), calls=%async_computation | async-start | bytes 2097152 | tf_op jit(solution)/shard_map/all_to_all | solution.py:36
  24.2 5.1 %fusion.3 = f32[1024]{0:T(1024)S(1)} fusion(bf16[1024,4096]{1,0:T(8,128)(2,1)} %param.11), kind=kLoop, calls=%fused_computation.7 | loop fusion | flops 12581888 | bytes 8392704 | tf_op jit(solution)/shard_map/reduce_sum | solution.py:27
  29.3 10.3 %fusion.5 = bf16[1024,4096]{1,0:T(8,128)(2,1)} fusion(bf16[1024,4096]{1,0:T(8,128)(2,1)} %param.11, f32[4096]{0:T(1024)S(1)} %copy-done.2, f32[1024]{0:T(1024)S(1)} %add_rsqrt_fusion), kind=kLoop, calls=%fused_computation.9 | loop fusion | flops 16777216 | bytes 16797696 | tf_op jit(solution)/shard_map/convert_element_type | solution.py:28
  39.6 8.5 %all-to-all-done = bf16[32,128,128]{2,1,0:T(8,128)(2,1)S(1)} async-done(((bf16[32,128,128]{2,1,0:T(8,128)(2,1)}), bf16[32,128,128]{2,1,0:T(8,128)(2,1)S(1)}, u32[]{:S(2)}, u32[]{:S(2)}) %all-to-all-start) | async-done | bytes 1048608 | tf_op jit(solution)/shard_map/all_to_all | solution.py:36
  48.1 5.7 %fusion.38 = (f32[128]{0:T(128)S(1)}, bf16[1024,128]{1,0:T(8,128)(2,1)S(1)}) fusion(bf16[1024,4096]{1,0:T(8,128)(2,1)} %fusion.5, bf16[4096,128]{1,0:T(8,128)(2,1)S(1)} %bitcast.94), kind=kOutput, calls=%fused_computation.57 | convolution fusion | flops 1074659200 | bytes 9699840 | tf_op jit(solution)/shard_map/dot_general | solution.py:32
  54.0 33.1 %all-gather.4.cloned.1.call-done = bf16[4096,128]{1,0:T(8,128)(2,1)} async-done(((bf16[128,128]{1,0:T(8,128)(2,1)}), bf16[4096,128]{1,0:T(8,128)(2,1)}) %all-gather.4.cloned.1.call-update) | async-done | bytes 1048592 | tf_op jit(solution)/shard_map/all_gather | solution.py:38
  87.1 5.9 %convolution_convert_fusion.2 = bf16[1024,128]{1,0:T(8,128)(2,1)S(1)} fusion(bf16[1024,4096]{1,0:T(8,128)(2,1)} %fusion.5, bf16[4096,128]{1,0:T(8,128)(2,1)} %all-gather.4.cloned.1.call-done), kind=kOutput, calls=%fused_computation.32 | convolution fusion | flops 1073872896 | bytes 9699328 | tf_op jit(solution)/shard_map/dot_general | solution.py:32
  94.0 254.0 %while.13 = (s32[]{:T(128)}, f32[1,128,128]{2,1,0:T(8,128)S(1)}, f32[1,128]{1,0:T(1,128)S(1)}, f32[1,128,128]{2,1,0:T(8,128)S(1)}, f32[1,128]{1,0:T(1,128)S(1)}, /*index=5*/s32[]{:T(128)}, s32[]{:T(128)}) while((s32[]{:T(128)}, f32[1,128,128]{2,1,0:T(8,128)S(1)}, f32[1,128]{1,0:T(1,128)S(1)}, f32[1,128,128]{2,1,0:T(8,128)S(1)}, ...), condition=%wide.region_4.5_spmd.clone, body=%wide.region_3.4_spmd.clone.sunk | while | flops 66051 | bytes 396456 | solution.py:64
  96.3 4.0 collective-permute-start.1
  107.3 4.0 collective-permute-start
  122.9 4.0 collective-permute-start
  146.4 4.0 collective-permute-start
  154.9 4.0 collective-permute-start
  158.9 4.0 collective-permute-start.1
  163.7 4.0 collective-permute-start
  172.0 4.0 collective-permute-start
  208.9 4.0 collective-permute-start.1
  225.6 4.0 collective-permute-start.1
  230.4 4.0 collective-permute-start
  234.4 4.1 collective-permute-start.1
  239.2 4.0 collective-permute-start
  243.2 4.0 collective-permute-start.1
  248.0 4.0 collective-permute-start
  259.6 4.8 collective-permute-start.1
  292.9 4.3 collective-permute-start.1
  309.8 4.1 collective-permute-start.1
  326.5 4.0 collective-permute-start.1
  334.8 4.0 collective-permute-start.1
  343.2 4.0 collective-permute-start.1
  348.1 9.1 %convolution_convert_fusion.1 = bf16[1024,512]{1,0:T(8,128)(2,1)S(1)} fusion(bf16[1024,4096]{1,0:T(8,128)(2,1)} %fusion.5, bf16[4096,512]{1,0:T(8,128)(2,1)} %all-gather.6.cloned.1.call-done), kind=kOutput, calls=%fused_computation.31 | convolution fusion | flops 4295491584 | bytes 13631488 | tf_op jit(solution)/shard_map/dot_general | solution.py:32
  370.7 8.9 %convolution_convert_fusion = bf16[1024,4096]{1,0:T(8,128)(2,1)} fusion(bf16[512,4096]{1,0:T(8,128)(2,1)} %all-gather.8.cloned.1.call-done, bf16[128,8,4,128]{3,2,1,0:T(4,128)(2,1)S(1)} %bitcast.95), kind=kOutput, calls=%fused_computation.13 | convolution fusion | flops 4299161600 | bytes 13631488 | tf_op jit(solution)/shard_map/dot_general | solution.py:94
  379.6 98.1 %reduce-scatter.2.cloned.1.call-done = bf16[1024,512]{1,0:T(8,128)(2,1)} async-done(((bf16[1024,4096]{1,0:T(8,128)(2,1)}), bf16[1024,512]{1,0:T(8,128)(2,1)}) %reduce-scatter.2.cloned.1.call-update) | async-done | bytes 1048592 | tf_op jit(solution)/shard_map/reduce_scatter | solution.py:97
  (275 shorter events, 187.5 us)
Async XLA Ops:
  6.5 80.6 %all-gather.4.cloned.1.call-start = ((), (), s32[]{:S(2)}) async-start(), calls=%async_computation.2 | async-start | bytes 1081344 | tf_op jit(solution)/shard_map/all_gather | solution.py:38
  7.3 340.8 %all-gather.6.cloned.1.call-start = ((), (), s32[]{:S(2)}) async-start(), calls=%async_computation.3 | async-start | bytes 4325376 | tf_op jit(solution)/shard_map/all_gather | solution.py:34
  10.0 38.1 %all-to-all-start = ((bf16[32,128,128]{2,1,0:T(8,128)(2,1)}), bf16[32,128,128]{2,1,0:T(8,128)(2,1)S(1)}, u32[]{:S(2)}, u32[]{:S(2)}) async-start(bf16[32,128,128]{2,1,0:T(8,128)(2,1)} %stack.2), calls=%async_computation | async-start | bytes 2097152 | tf_op jit(solution)/shard_map/all_to_all | solution.py:36
  22.0 348.7 %all-gather.8.cloned.1.call-start = ((), (), s32[]{:S(2)}) async-start(), calls=%async_computation.4 | async-start | bytes 4325376 | tf_op jit(solution)/shard_map/all_gather | solution.py:95
  22.8 455.0 %reduce-scatter.2.cloned.1.call-start = ((), (), s32[]{:S(2)}) async-start(), calls=%async_computation.5 | async-start | bytes 9437184 | tf_op jit(solution)/shard_map/reduce_scatter | solution.py:97
  107.3 8.1 %collective-permute-start = (bf16[1,128,128]{2,1,0:T(8,128)(2,1)S(1)}, bf16[1,128,128]{2,1,0:T(8,128)(2,1)S(1)}, u32[]{:S(2)}, u32[]{:S(2)}) collective-permute-start(bf16[1,128,128]{2,1,0:T(8,128)(2,1)S(1)} %fusion.74), channel_id=1, source_target_pairs={{0,8},{8,16},{16,24},{24,32},{32,40},{40,48},{48,56},{56,64},{64,7... | collective-permute-start | bytes 98312 | tf_op jit(solution)/shard_map/while/body/eval_jaxpr/ppermute | solution.py:16
  122.9 8.1 %collective-permute-start = (bf16[1,128,128]{2,1,0:T(8,128)(2,1)S(1)}, bf16[1,128,128]{2,1,0:T(8,128)(2,1)S(1)}, u32[]{:S(2)}, u32[]{:S(2)}) collective-permute-start(bf16[1,128,128]{2,1,0:T(8,128)(2,1)S(1)} %fusion.74), channel_id=1, source_target_pairs={{0,8},{8,16},{16,24},{24,32},{32,40},{40,48},{48,56},{56,64},{64,7... | collective-permute-start | bytes 98312 | tf_op jit(solution)/shard_map/while/body/eval_jaxpr/ppermute | solution.py:16
  131.0 7.8 %collective-permute-start = (bf16[1,128,128]{2,1,0:T(8,128)(2,1)S(1)}, bf16[1,128,128]{2,1,0:T(8,128)(2,1)S(1)}, u32[]{:S(2)}, u32[]{:S(2)}) collective-permute-start(bf16[1,128,128]{2,1,0:T(8,128)(2,1)S(1)} %fusion.74), channel_id=1, source_target_pairs={{0,8},{8,16},{16,24},{24,32},{32,40},{40,48},{48,56},{56,64},{64,7... | collective-permute-start | bytes 98312 | tf_op jit(solution)/shard_map/while/body/eval_jaxpr/ppermute | solution.py:16
  146.4 8.5 %collective-permute-start = (bf16[1,128,128]{2,1,0:T(8,128)(2,1)S(1)}, bf16[1,128,128]{2,1,0:T(8,128)(2,1)S(1)}, u32[]{:S(2)}, u32[]{:S(2)}) collective-permute-start(bf16[1,128,128]{2,1,0:T(8,128)(2,1)S(1)} %fusion.74), channel_id=1, source_target_pairs={{0,8},{8,16},{16,24},{24,32},{32,40},{40,48},{48,56},{56,64},{64,7... | collective-permute-start | bytes 98312 | tf_op jit(solution)/shard_map/while/body/eval_jaxpr/ppermute | solution.py:16
  154.9 8.7 %collective-permute-start = (bf16[1,128,128]{2,1,0:T(8,128)(2,1)S(1)}, bf16[1,128,128]{2,1,0:T(8,128)(2,1)S(1)}, u32[]{:S(2)}, u32[]{:S(2)}) collective-permute-start(bf16[1,128,128]{2,1,0:T(8,128)(2,1)S(1)} %fusion.74), channel_id=1, source_target_pairs={{0,8},{8,16},{16,24},{24,32},{32,40},{40,48},{48,56},{56,64},{64,7... | collective-permute-start | bytes 98312 | tf_op jit(solution)/shard_map/while/body/eval_jaxpr/ppermute | solution.py:16
  163.7 8.3 %collective-permute-start = (bf16[1,128,128]{2,1,0:T(8,128)(2,1)S(1)}, bf16[1,128,128]{2,1,0:T(8,128)(2,1)S(1)}, u32[]{:S(2)}, u32[]{:S(2)}) collective-permute-start(bf16[1,128,128]{2,1,0:T(8,128)(2,1)S(1)} %fusion.74), channel_id=1, source_target_pairs={{0,8},{8,16},{16,24},{24,32},{32,40},{40,48},{48,56},{56,64},{64,7... | collective-permute-start | bytes 98312 | tf_op jit(solution)/shard_map/while/body/eval_jaxpr/ppermute | solution.py:16
  172.0 8.3 %collective-permute-start = (bf16[1,128,128]{2,1,0:T(8,128)(2,1)S(1)}, bf16[1,128,128]{2,1,0:T(8,128)(2,1)S(1)}, u32[]{:S(2)}, u32[]{:S(2)}) collective-permute-start(bf16[1,128,128]{2,1,0:T(8,128)(2,1)S(1)} %fusion.74), channel_id=1, source_target_pairs={{0,8},{8,16},{16,24},{24,32},{32,40},{40,48},{48,56},{56,64},{64,7... | collective-permute-start | bytes 98312 | tf_op jit(solution)/shard_map/while/body/eval_jaxpr/ppermute | solution.py:16
  180.3 8.4 %collective-permute-start = (bf16[1,128,128]{2,1,0:T(8,128)(2,1)S(1)}, bf16[1,128,128]{2,1,0:T(8,128)(2,1)S(1)}, u32[]{:S(2)}, u32[]{:S(2)}) collective-permute-start(bf16[1,128,128]{2,1,0:T(8,128)(2,1)S(1)} %fusion.74), channel_id=1, source_target_pairs={{0,8},{8,16},{16,24},{24,32},{32,40},{40,48},{48,56},{56,64},{64,7... | collective-permute-start | bytes 98312 | tf_op jit(solution)/shard_map/while/body/eval_jaxpr/ppermute | solution.py:16
  188.7 8.3 %collective-permute-start = (bf16[1,128,128]{2,1,0:T(8,128)(2,1)S(1)}, bf16[1,128,128]{2,1,0:T(8,128)(2,1)S(1)}, u32[]{:S(2)}, u32[]{:S(2)}) collective-permute-start(bf16[1,128,128]{2,1,0:T(8,128)(2,1)S(1)} %fusion.74), channel_id=1, source_target_pairs={{0,8},{8,16},{16,24},{24,32},{32,40},{40,48},{48,56},{56,64},{64,7... | collective-permute-start | bytes 98312 | tf_op jit(solution)/shard_map/while/body/eval_jaxpr/ppermute | solution.py:16
  197.1 7.9 %collective-permute-start = (bf16[1,128,128]{2,1,0:T(8,128)(2,1)S(1)}, bf16[1,128,128]{2,1,0:T(8,128)(2,1)S(1)}, u32[]{:S(2)}, u32[]{:S(2)}) collective-permute-start(bf16[1,128,128]{2,1,0:T(8,128)(2,1)S(1)} %fusion.74), channel_id=1, source_target_pairs={{0,8},{8,16},{16,24},{24,32},{32,40},{40,48},{48,56},{56,64},{64,7... | collective-permute-start | bytes 98312 | tf_op jit(solution)/shard_map/while/body/eval_jaxpr/ppermute | solution.py:16
  205.0 8.6 %collective-permute-start = (bf16[1,128,128]{2,1,0:T(8,128)(2,1)S(1)}, bf16[1,128,128]{2,1,0:T(8,128)(2,1)S(1)}, u32[]{:S(2)}, u32[]{:S(2)}) collective-permute-start(bf16[1,128,128]{2,1,0:T(8,128)(2,1)S(1)} %fusion.74), channel_id=1, source_target_pairs={{0,8},{8,16},{16,24},{24,32},{32,40},{40,48},{48,56},{56,64},{64,7... | collective-permute-start | bytes 98312 | tf_op jit(solution)/shard_map/while/body/eval_jaxpr/ppermute | solution.py:16
  213.6 8.3 %collective-permute-start = (bf16[1,128,128]{2,1,0:T(8,128)(2,1)S(1)}, bf16[1,128,128]{2,1,0:T(8,128)(2,1)S(1)}, u32[]{:S(2)}, u32[]{:S(2)}) collective-permute-start(bf16[1,128,128]{2,1,0:T(8,128)(2,1)S(1)} %fusion.74), channel_id=1, source_target_pairs={{0,8},{8,16},{16,24},{24,32},{32,40},{40,48},{48,56},{56,64},{64,7... | collective-permute-start | bytes 98312 | tf_op jit(solution)/shard_map/while/body/eval_jaxpr/ppermute | solution.py:16
  222.0 8.4 %collective-permute-start = (bf16[1,128,128]{2,1,0:T(8,128)(2,1)S(1)}, bf16[1,128,128]{2,1,0:T(8,128)(2,1)S(1)}, u32[]{:S(2)}, u32[]{:S(2)}) collective-permute-start(bf16[1,128,128]{2,1,0:T(8,128)(2,1)S(1)} %fusion.74), channel_id=1, source_target_pairs={{0,8},{8,16},{16,24},{24,32},{32,40},{40,48},{48,56},{56,64},{64,7... | collective-permute-start | bytes 98312 | tf_op jit(solution)/shard_map/while/body/eval_jaxpr/ppermute | solution.py:16
  230.4 8.8 %collective-permute-start = (bf16[1,128,128]{2,1,0:T(8,128)(2,1)S(1)}, bf16[1,128,128]{2,1,0:T(8,128)(2,1)S(1)}, u32[]{:S(2)}, u32[]{:S(2)}) collective-permute-start(bf16[1,128,128]{2,1,0:T(8,128)(2,1)S(1)} %fusion.74), channel_id=1, source_target_pairs={{0,8},{8,16},{16,24},{24,32},{32,40},{40,48},{48,56},{56,64},{64,7... | collective-permute-start | bytes 98312 | tf_op jit(solution)/shard_map/while/body/eval_jaxpr/ppermute | solution.py:16
  239.2 8.7 %collective-permute-start = (bf16[1,128,128]{2,1,0:T(8,128)(2,1)S(1)}, bf16[1,128,128]{2,1,0:T(8,128)(2,1)S(1)}, u32[]{:S(2)}, u32[]{:S(2)}) collective-permute-start(bf16[1,128,128]{2,1,0:T(8,128)(2,1)S(1)} %fusion.74), channel_id=1, source_target_pairs={{0,8},{8,16},{16,24},{24,32},{32,40},{40,48},{48,56},{56,64},{64,7... | collective-permute-start | bytes 98312 | tf_op jit(solution)/shard_map/while/body/eval_jaxpr/ppermute | solution.py:16
  248.0 8.0 %collective-permute-start = (bf16[1,128,128]{2,1,0:T(8,128)(2,1)S(1)}, bf16[1,128,128]{2,1,0:T(8,128)(2,1)S(1)}, u32[]{:S(2)}, u32[]{:S(2)}) collective-permute-start(bf16[1,128,128]{2,1,0:T(8,128)(2,1)S(1)} %fusion.74), channel_id=1, source_target_pairs={{0,8},{8,16},{16,24},{24,32},{32,40},{40,48},{48,56},{56,64},{64,7... | collective-permute-start | bytes 98312 | tf_op jit(solution)/shard_map/while/body/eval_jaxpr/ppermute | solution.py:16
  256.0 9.1 %collective-permute-start = (bf16[1,128,128]{2,1,0:T(8,128)(2,1)S(1)}, bf16[1,128,128]{2,1,0:T(8,128)(2,1)S(1)}, u32[]{:S(2)}, u32[]{:S(2)}) collective-permute-start(bf16[1,128,128]{2,1,0:T(8,128)(2,1)S(1)} %fusion.74), channel_id=1, source_target_pairs={{0,8},{8,16},{16,24},{24,32},{32,40},{40,48},{48,56},{56,64},{64,7... | collective-permute-start | bytes 98312 | tf_op jit(solution)/shard_map/while/body/eval_jaxpr/ppermute | solution.py:16
  265.1 8.2 %collective-permute-start = (bf16[1,128,128]{2,1,0:T(8,128)(2,1)S(1)}, bf16[1,128,128]{2,1,0:T(8,128)(2,1)S(1)}, u32[]{:S(2)}, u32[]{:S(2)}) collective-permute-start(bf16[1,128,128]{2,1,0:T(8,128)(2,1)S(1)} %fusion.74), channel_id=1, source_target_pairs={{0,8},{8,16},{16,24},{24,32},{32,40},{40,48},{48,56},{56,64},{64,7... | collective-permute-start | bytes 98312 | tf_op jit(solution)/shard_map/while/body/eval_jaxpr/ppermute | solution.py:16
  273.4 7.8 %collective-permute-start = (bf16[1,128,128]{2,1,0:T(8,128)(2,1)S(1)}, bf16[1,128,128]{2,1,0:T(8,128)(2,1)S(1)}, u32[]{:S(2)}, u32[]{:S(2)}) collective-permute-start(bf16[1,128,128]{2,1,0:T(8,128)(2,1)S(1)} %fusion.74), channel_id=1, source_target_pairs={{0,8},{8,16},{16,24},{24,32},{32,40},{40,48},{48,56},{56,64},{64,7... | collective-permute-start | bytes 98312 | tf_op jit(solution)/shard_map/while/body/eval_jaxpr/ppermute | solution.py:16
  281.2 8.0 %collective-permute-start = (bf16[1,128,128]{2,1,0:T(8,128)(2,1)S(1)}, bf16[1,128,128]{2,1,0:T(8,128)(2,1)S(1)}, u32[]{:S(2)}, u32[]{:S(2)}) collective-permute-start(bf16[1,128,128]{2,1,0:T(8,128)(2,1)S(1)} %fusion.74), channel_id=1, source_target_pairs={{0,8},{8,16},{16,24},{24,32},{32,40},{40,48},{48,56},{56,64},{64,7... | collective-permute-start | bytes 98312 | tf_op jit(solution)/shard_map/while/body/eval_jaxpr/ppermute | solution.py:16
  289.3 8.6 %collective-permute-start = (bf16[1,128,128]{2,1,0:T(8,128)(2,1)S(1)}, bf16[1,128,128]{2,1,0:T(8,128)(2,1)S(1)}, u32[]{:S(2)}, u32[]{:S(2)}) collective-permute-start(bf16[1,128,128]{2,1,0:T(8,128)(2,1)S(1)} %fusion.74), channel_id=1, source_target_pairs={{0,8},{8,16},{16,24},{24,32},{32,40},{40,48},{48,56},{56,64},{64,7... | collective-permute-start | bytes 98312 | tf_op jit(solution)/shard_map/while/body/eval_jaxpr/ppermute | solution.py:16
  298.0 8.2 %collective-permute-start = (bf16[1,128,128]{2,1,0:T(8,128)(2,1)S(1)}, bf16[1,128,128]{2,1,0:T(8,128)(2,1)S(1)}, u32[]{:S(2)}, u32[]{:S(2)}) collective-permute-start(bf16[1,128,128]{2,1,0:T(8,128)(2,1)S(1)} %fusion.74), channel_id=1, source_target_pairs={{0,8},{8,16},{16,24},{24,32},{32,40},{40,48},{48,56},{56,64},{64,7... | collective-permute-start | bytes 98312 | tf_op jit(solution)/shard_map/while/body/eval_jaxpr/ppermute | solution.py:16
  306.2 8.4 %collective-permute-start = (bf16[1,128,128]{2,1,0:T(8,128)(2,1)S(1)}, bf16[1,128,128]{2,1,0:T(8,128)(2,1)S(1)}, u32[]{:S(2)}, u32[]{:S(2)}) collective-permute-start(bf16[1,128,128]{2,1,0:T(8,128)(2,1)S(1)} %fusion.74), channel_id=1, source_target_pairs={{0,8},{8,16},{16,24},{24,32},{32,40},{40,48},{48,56},{56,64},{64,7... | collective-permute-start | bytes 98312 | tf_op jit(solution)/shard_map/while/body/eval_jaxpr/ppermute | solution.py:16
  314.6 8.2 %collective-permute-start = (bf16[1,128,128]{2,1,0:T(8,128)(2,1)S(1)}, bf16[1,128,128]{2,1,0:T(8,128)(2,1)S(1)}, u32[]{:S(2)}, u32[]{:S(2)}) collective-permute-start(bf16[1,128,128]{2,1,0:T(8,128)(2,1)S(1)} %fusion.74), channel_id=1, source_target_pairs={{0,8},{8,16},{16,24},{24,32},{32,40},{40,48},{48,56},{56,64},{64,7... | collective-permute-start | bytes 98312 | tf_op jit(solution)/shard_map/while/body/eval_jaxpr/ppermute | solution.py:16
  322.9 8.3 %collective-permute-start = (bf16[1,128,128]{2,1,0:T(8,128)(2,1)S(1)}, bf16[1,128,128]{2,1,0:T(8,128)(2,1)S(1)}, u32[]{:S(2)}, u32[]{:S(2)}) collective-permute-start(bf16[1,128,128]{2,1,0:T(8,128)(2,1)S(1)} %fusion.74), channel_id=1, source_target_pairs={{0,8},{8,16},{16,24},{24,32},{32,40},{40,48},{48,56},{56,64},{64,7... | collective-permute-start | bytes 98312 | tf_op jit(solution)/shard_map/while/body/eval_jaxpr/ppermute | solution.py:16
  331.2 8.3 %collective-permute-start = (bf16[1,128,128]{2,1,0:T(8,128)(2,1)S(1)}, bf16[1,128,128]{2,1,0:T(8,128)(2,1)S(1)}, u32[]{:S(2)}, u32[]{:S(2)}) collective-permute-start(bf16[1,128,128]{2,1,0:T(8,128)(2,1)S(1)} %fusion.74), channel_id=1, source_target_pairs={{0,8},{8,16},{16,24},{24,32},{32,40},{40,48},{48,56},{56,64},{64,7... | collective-permute-start | bytes 98312 | tf_op jit(solution)/shard_map/while/body/eval_jaxpr/ppermute | solution.py:16
  339.6 8.3 %collective-permute-start = (bf16[1,128,128]{2,1,0:T(8,128)(2,1)S(1)}, bf16[1,128,128]{2,1,0:T(8,128)(2,1)S(1)}, u32[]{:S(2)}, u32[]{:S(2)}) collective-permute-start(bf16[1,128,128]{2,1,0:T(8,128)(2,1)S(1)} %fusion.74), channel_id=1, source_target_pairs={{0,8},{8,16},{16,24},{24,32},{32,40},{40,48},{48,56},{56,64},{64,7... | collective-permute-start | bytes 98312 | tf_op jit(solution)/shard_map/while/body/eval_jaxpr/ppermute | solution.py:16
  (43 other events, 1337.8 us)
Sparse Core Ops, SparseCore 0:
  9.9 77.1 all-gather.3
  89.7 81.8 all-gather.5
  174.1 82.8 all-gather.7
  379.8 97.9 reduce-scatter.1
